TPU v7x, 32 devices: a whole 2x2x4 slice. The times are simulated.
32 devices in a mesh: guide: 2 (over core), blk: 16 (over z, y, x).
Axes of the slice: x: 2, y: 2, z: 4, core: 2. Of those that a mesh axis runs over, the one named last changes fastest.
Arguments:
- x_cols: bfloat16 [128, 2048], P(None, 'blk'), may hold values from -3 to 3
- queries: bfloat16 [128, 9216], P('blk'), may hold values from -64 to 64
- new_kv: bfloat16 [128, 576], P('blk'), may hold values from -6 to 6
- cache: bfloat16 [2, 128, 256, 576], P('guide', 'blk'), may hold values from -8 to 8
- lengths: int32 [2, 128], P('guide'), may hold values from 2 to 256, as said below
- perm: int32 [128], replicated, may hold values from 0 to 127, each once
- guide_scale: float32 [128], replicated, may hold values from 1.5 to 7.5
- w_uv: bfloat16 [16, 512, 128], replicated, may hold values from -0.75 to 0.75
- w_out: bfloat16 [2048, 2048], P(None, 'blk'), may hold values from -0.125 to 0.125
- mlp_gain: float32 [2048], replicated, may hold values from 0.5 to 1.5
- w_gate: bfloat16 [2048, 10944], P(None, 'blk'), may hold values from -0.125 to 0.125
- w_up: bfloat16 [2048, 10944], P(None, 'blk'), may hold values from -0.125 to 0.125
- w_down: bfloat16 [10944, 2048], P('blk'), may hold values from -0.0546875 to 0.0546875
- head_gain: float32 [2048], replicated, may hold values from 0.5 to 1.5
- w_head: bfloat16 [2048, 102400], P(None, 'blk'), may hold values from -0.125 to 0.125
Outputs:
- guided: bfloat16 [128, 102400], P('guide', 'blk')
Inputs may be any that keep to these rules, and one draw needn't show every extreme that they name: Positions 0 to lengths[g, r] - 1 of request r's cache in group g are live; each group has a request with 256 live positions. Slot s holds request perm[s]; every request has one slot.
All inputs are finite; a program needn't handle non-finite values.
Results may differ from a plain program's by a relative error of at most 0.018.
Values may be sent and summed in bfloat16 or wider, within the bound.
No kernel may reach another device: no remote copies, remote signals or barrier semaphores. Data moves between devices by JAX's collectives and lax.ppermute only.
A program may use at most 128 MiB of HBM per device.

v0:
```python
import jax
import jax.numpy as jnp
from jax import lax
from jax.sharding import PartitionSpec as P

FF = 10944


def partner(value, axis, apart):
    mask = 2**apart
    pairs = [(source, source ^ mask) for source in range(lax.axis_size(axis))]
    return lax.ppermute(value, axis, pairs)


def rms_round(hidden, gain):
    values = hidden.astype(jnp.float32)
    meansq = jnp.mean(values * values, axis=-1, keepdims=True)
    return (values * lax.rsqrt(meansq + 1e-06) * gain).astype(jnp.bfloat16)


def body(
    x_cols,
    queries,
    new_kv,
    cache,
    lengths,
    perm,
    guide_scale,
    w_uv,
    w_out,
    mlp_gain,
    w_gate,
    w_up,
    w_down,
    head_gain,
    w_head,
):
    guide_index = lax.axis_index("guide")
    blk_index = lax.axis_index("blk")
    slots_dev = queries.shape[0]
    heads_count = w_uv.shape[0]
    latent_size = w_uv.shape[1]
    key_width = new_kv.shape[1]
    score_scale = (w_uv.shape[2] + key_width - latent_size) ** (-0.5)
    slot_ids = blk_index * slots_dev + jnp.arange(slots_dev, dtype=jnp.int32)
    owners = jnp.take(perm, slot_ids)
    live_len = jnp.take(lengths[0], owners)
    query_heads = queries.reshape(slots_dev, heads_count, key_width)
    cached_keys = cache[0]
    scores = (
        jnp.einsum("shk,slk->shl", query_heads, cached_keys, preferred_element_type=jnp.float32)
        * score_scale
    )
    own_score = (
        jnp.einsum("shk,sk->sh", query_heads, new_kv, preferred_element_type=jnp.float32)
        * score_scale
    )
    live_mask = (
        jnp.arange(cached_keys.shape[1], dtype=jnp.int32)[None, None, :] < live_len[:, None, None]
    )
    scores = jnp.where(live_mask, scores, jnp.float32(-1e30))
    peak_score = jnp.maximum(jnp.max(scores, axis=-1), own_score)
    probs = jnp.where(live_mask, jnp.exp(scores - peak_score[..., None]), jnp.float32(0.0))
    own_prob = jnp.exp(own_score - peak_score)
    softmax_total = jnp.sum(probs, axis=-1) + own_prob
    weights = (probs / softmax_total[..., None]).astype(jnp.bfloat16)
    own_weight = (own_prob / softmax_total).astype(jnp.bfloat16)
    latent_out = jnp.einsum(
        "shl,slc->shc", weights, cached_keys[:, :, :latent_size], preferred_element_type=jnp.float32
    )
    latent_out = latent_out + own_weight.astype(jnp.float32)[..., None] * new_kv[
        :, None, :latent_size
    ].astype(jnp.float32)
    value_rows = jnp.einsum(
        "shc,hcd->shd", latent_out.astype(jnp.bfloat16), w_uv, preferred_element_type=jnp.float32
    )
    value_rows = value_rows.astype(jnp.bfloat16).reshape(slots_dev, -1)
    attended = jnp.dot(
        lax.all_gather(value_rows, "blk", axis=0, tiled=True),
        w_out,
        preferred_element_type=jnp.float32,
    )
    residual = (x_cols.astype(jnp.float32) + attended).astype(jnp.bfloat16)
    rows_full = lax.all_gather(residual, "blk", axis=1, tiled=True)
    normed = rms_round(rows_full, mlp_gain)
    unit_count = w_gate.shape[1]
    gate_out = jnp.dot(normed, w_gate, preferred_element_type=jnp.float32)
    up_out = jnp.dot(normed, w_up, preferred_element_type=jnp.float32)
    unit_ids = blk_index * unit_count + jnp.arange(unit_count, dtype=jnp.int32)
    hidden = jnp.where(
        unit_ids[None, :] < FF, jax.nn.silu(gate_out) * up_out, jnp.float32(0.0)
    ).astype(jnp.bfloat16)
    partial_sum = jnp.dot(hidden, w_down, preferred_element_type=jnp.float32)
    summed = lax.psum(partial_sum, "blk")
    after_mlp = (rows_full.astype(jnp.float32) + summed).astype(jnp.bfloat16)
    logits = jnp.dot(rms_round(after_mlp, head_gain), w_head, preferred_element_type=jnp.float32)
    request_count = logits.shape[0]
    half_rows = request_count // 2
    slot_scale = jnp.take(guide_scale, perm)
    request_order = (
        jnp.zeros((request_count,), jnp.int32)
        .at[perm]
        .set(jnp.arange(request_count, dtype=jnp.int32))
    )
    own_order = lax.dynamic_slice_in_dim(request_order, guide_index * half_rows, half_rows)
    other_logits = partner(logits.astype(jnp.bfloat16), "guide", 0).astype(logits.dtype)
    cond_logits = jnp.where(guide_index == 0, logits, other_logits)
    uncond_logits = jnp.where(guide_index == 0, other_logits, logits)
    mixed = (uncond_logits + slot_scale[:, None] * (cond_logits - uncond_logits)).astype(
        jnp.bfloat16
    )
    return jnp.take(mixed, own_order, axis=0)


def solution(mesh):
    return jax.shard_map(
        body,
        mesh=mesh,
        in_specs=(
            P(None, "blk"),
            P("blk", None),
            P("blk", None),
            P("guide", "blk", None, None),
            P("guide", None),
            P(),
            P(),
            P(),
            P(None, "blk"),
            P(),
            P(None, "blk"),
            P(None, "blk"),
            P("blk", None),
            P(),
            P(None, "blk"),
        ),
        out_specs=P("guide", "blk"),
        check_vma=False,
    )
```

profile of v0, /device:TPU:0, one launch (start us, length us, event | category | flops | bytes accessed | tf_op | source)
XLA Modules:
  0.0 257.7 jit_solution(10083849745343940406)
XLA Ops:
  6.5 0.0 all-reduce.2.cloned.1.call-start
  6.5 1.2 reshape.73
  7.8 1.3 gather_fusion.2
  9.1 1.3 gather_fusion.3
  10.4 0.1 iota_compare_fusion
  10.5 0.7 slice_convert_fusion
  11.2 0.9 fusion.44
  12.1 2.2 fusion.55
  14.3 0.2 fusion.39
  14.5 0.1 copy.17
  14.6 2.4 fusion.4
  17.0 0.5 fusion.11
  17.5 45.3 %all_gather.6 = bf16[128,2048]{1,0:T(8,128)(2,1)S(1)} all-gather(bf16[8,2048]{1,0:T(8,128)(2,1)S(1)} %fusion.11), channel_id=1, replica_groups=mesh['guide'=2,'blk'=16] {'blk'}, dimensions={0}, use_global_device_ids=true | all-gather | bytes 557056 | tf_op jit(solution)/shard_map/all_gather | solution.py:79
  62.8 0.3 fusion.10
  63.1 38.5 %all_gather.7 = bf16[128,2048]{1,0:T(8,128)(2,1)S(1)} all-gather(bf16[128,128]{1,0:T(8,128)(2,1)S(1)} %fusion.10), channel_id=1, replica_groups=mesh['guide'=2,'blk'=16] {'blk'}, dimensions={1}, use_global_device_ids=true | all-gather | bytes 557056 | tf_op jit(solution)/shard_map/all_gather | solution.py:84
  101.7 0.2 fusion.15
  101.9 3.5 %fusion.34 = f32[128,684]{0,1:T(8,128)} fusion(bf16[2048,684]{0,1:T(8,128)(2,1)} %param.27, bf16[128,2048]{1,0:T(8,128)(2,1)S(1)} %all_gather.7, f32[2048]{0:T(1024)S(1)} %copy-done.7, f32[128]{0:T(128)S(1)} %add_rsqrt_fusion.1), kind=kOutput, calls=%fused_computation.49 | convolution fusion | flops 359661568 | bytes 3684864 | tf_op jit(solution)/shard_map/dot_general | solution.py:87
  105.4 5.0 %fusion.8 = f32[128,2048]{1,0:T(8,128)} fusion(bf16[684,2048]{1,0:T(8,128)(2,1)S(1)} %copy-done, bf16[2048,684]{0,1:T(8,128)(2,1)} %param.28, f32[128,684]{0,1:T(8,128)} %fusion.34, pred[684]{0:T(1024)(128)(4,1)S(1)} %add_compare_fusion, bf16[128,2048]{1,0:T(8,128)(2,1)S(1)} %all_gather.7, f32[2048]{0:T(1024)S(1)} %copy-done.7, f32[128]{0:T(128)S(1)} %add_rsqrt_fusion.1), kind=kOutput, calls=%fused_computation.21 | convolution fusion | flops 718887424 | bytes 7535788 | tf_op jit(solution)/shard_map/dot_general | solution.py:93
  110.4 0.0 all-reduce.2.cloned.1.call-update
  110.5 109.6 %all-reduce.2.cloned.1.call-done = f32[128,2048]{1,0:T(8,128)} async-done(((f32[128,2048]{1,0:T(8,128)}), f32[128,2048]{1,0:T(8,128)}) %all-reduce.2.cloned.1.call-update) | async-done | bytes 1048592 | tf_op jit(solution)/shard_map/psum | solution.py:94
  220.1 1.4 fusion.12
  221.5 0.0 copy-start.2
  221.5 0.0 copy-start.1
  221.5 14.7 %fusion.56 = (bf16[128,6400]{1,0:T(8,128)(2,1)}, f32[128,6400]{1,0:T(8,128)}) fusion(bf16[2048,6400]{1,0:T(8,128)(2,1)} %param.31, f32[2048]{0:T(1024)S(1)} %copy-done.5, f32[128]{0:T(128)S(1)} %add_rsqrt_fusion, f32[128,2048]{1,0:T(8,128)} %all-reduce.2.cloned.1.call-done, bf16[128,2048]{1,0:T(8,128)(2,1)S(1)} %all_gather.7), kind=kOutput, calls=%fused_computation.90 | convolution fusion | flops 3358097408 | bytes 32711168 | tf_op jit(solution)/shard_map/dot_general | solution.py:96
  236.2 0.0 collective-permute-start
  236.2 1.2 scatter_custom_fusion
  237.4 1.2 gather_fusion
  238.6 0.1 compare_and_fusion
  238.8 1.3 collective-permute-done
  240.1 4.3 %fusion.3 = bf16[128,6400]{1,0:T(8,128)(2,1)} fusion(f32[128,6400]{1,0:T(8,128)} %get-tuple-element.13, bf16[128,6400]{1,0:T(8,128)(2,1)} %collective-permute-done, f32[128]{0:T(128)S(1)} %and_select_fusion.2, pred[]{:T(512)S(6)} %eq.4), kind=kLoop, calls=%fused_computation.10 | loop fusion | flops 5734400 | bytes 6554113 | tf_op jit(solution)/shard_map/convert_element_type | solution.py:109
  244.4 4.3 %gather_fusion.1 = bf16[64,6400]{1,0:T(8,128)(2,1)} fusion(bf16[128,6400]{1,0:T(8,128)(2,1)} %fusion.3, s32[1024]{0:T(1024)S(1)} %pad_clamp_fusion), kind=kCustom, calls=%fused_computation.3 | custom fusion | bytes 1638656 | tf_op jit(solution)/shard_map/jit(_take)/gather | solution.py:112
  248.7 2.2 broadcast_select_fusion
  (29 shorter events, 0.1 us)
Async XLA Ops:
  6.5 98.9 %copy-start = (bf16[684,2048]{1,0:T(8,128)(2,1)S(1)}, bf16[684,2048]{1,0:T(8,128)(2,1)}, u32[]{:S(2)}) copy-start(bf16[684,2048]{1,0:T(8,128)(2,1)} %param.29) | copy-start | bytes 8404996
  6.5 213.5 %all-reduce.2.cloned.1.call-start = ((), (), s32[]{:S(2)}) async-start(), calls=%async_computation | async-start | bytes 2097152 | tf_op jit(solution)/shard_map/psum | solution.py:94
  14.6 2.4 copy-start.3
  14.6 48.3 %copy-start.4 = (bf16[2048,128]{1,0:T(8,128)(2,1)S(1)}, bf16[2048,128]{1,0:T(8,128)(2,1)}, u32[]{:S(2)}) copy-start(bf16[2048,128]{1,0:T(8,128)(2,1)} %param.25) | copy-start | bytes 1572868
  14.6 48.3 %copy-start.6 = (bf16[128,128]{1,0:T(8,128)(2,1)S(1)}, bf16[128,128]{1,0:T(8,128)(2,1)}, u32[]{:S(2)}) copy-start(bf16[128,128]{1,0:T(8,128)(2,1)} %param.17) | copy-start | bytes 98308
  17.0 84.9 %copy-start.7 = (f32[2048]{0:T(1024)S(1)}, f32[2048]{0:T(1024)}, u32[]{:S(2)}) copy-start(f32[2048]{0:T(1024)} %param.26) | copy-start | bytes 24580
  105.4 116.1 %copy-start.5 = (f32[2048]{0:T(1024)S(1)}, f32[2048]{0:T(1024)}, u32[]{:S(2)}) copy-start(f32[2048]{0:T(1024)} %param.30) | copy-start | bytes 24580
  221.5 14.7 %copy-start.2 = (s32[128]{0:T(128)S(1)}, s32[128]{0:T(128)}, u32[]{:S(2)}) copy-start(s32[128]{0:T(128)} %param.22) | copy-start | bytes 1540
  221.5 15.9 %copy-start.1 = (f32[128]{0:T(128)S(1)}, f32[128]{0:T(128)}, u32[]{:S(2)}) copy-start(f32[128]{0:T(128)} %param.23) | copy-start | bytes 1540
  236.2 3.8 %collective-permute-start = (bf16[128,6400]{1,0:T(8,128)(2,1)}, bf16[128,6400]{1,0:T(8,128)(2,1)}, u32[]{:S(2)}, u32[]{:S(2)}) collective-permute-start(bf16[128,6400]{1,0:T(8,128)(2,1)} %get-tuple-element.12), channel_id=1, source_target_pairs={{0,16},{16,0},{1,17},{17,1},{2,18},{18,2},{3,19},{19,3},{4,20},{20... | collective-permute-start | bytes 4915208 | tf_op jit(solution)/shard_map/ppermute | solution.py:12
Sparse Core Ops, SparseCore 0:
  110.6 109.4 all-reduce.1
where the time goes:
time: 258 us
  waiting for transfers between devices  111 us (43%)
  blocking collectives  83.9 us (33%)
  matrix products  29.5 us (11%)
  between operations  13.5 us (5%)
  local copies, waits for them, and re-layouts  10.7 us (4%)
  other arithmetic  9.26 us (4%)
    psum x1, waiting for transfers between devices, body(): summed = lax.psum(partial_sum, 'blk')  110 us
    all_gather x1, blocking collectives, body(): lax.all_gather(value_rows, 'blk', axis=0, tiled=True)  45.3 us
    all_gather x1, blocking collectives, body(): rows_full = lax.all_gather(residual, 'blk', axis=1, tiled=True)  38.5 us
    dot_general x1, matrix products, body(): jnp.dot(rms_round(after_mlp, head_gain), w_head, preferred_element_type=j...  14.7 us
  transfers between devices with their start and end apart: 2, of which 2 were waited for; matrix products, arithmetic and copies ran while one was open for 1% of the time, Pallas kernels for 0%

commit v1 on v0

--- a/solution.py
+++ b/solution.py
@@ -4,6 +4,18 @@
 from jax.sharding import PartitionSpec as P
 
 FF = 10944
+
+
+def collect(x, axis, dim):
+    ways, here = (lax.axis_size(axis), lax.axis_index(axis))
+    grown, reach = (x, 1)
+    while reach < ways:
+        theirs = lax.ppermute(grown, axis, [(d, d ^ reach) for d in range(ways)])
+        mine_first = jnp.concatenate([grown, theirs], axis=dim)
+        theirs_first = jnp.concatenate([theirs, grown], axis=dim)
+        grown = jnp.where(here & reach == 0, mine_first, theirs_first)
+        reach = 2 * reach
+    return grown
 
 
 def partner(value, axis, apart):
@@ -75,11 +87,7 @@
         "shc,hcd->shd", latent_out.astype(jnp.bfloat16), w_uv, preferred_element_type=jnp.float32
     )
     value_rows = value_rows.astype(jnp.bfloat16).reshape(slots_dev, -1)
-    attended = jnp.dot(
-        lax.all_gather(value_rows, "blk", axis=0, tiled=True),
-        w_out,
-        preferred_element_type=jnp.float32,
-    )
+    attended = jnp.dot(collect(value_rows, "blk", 0), w_out, preferred_element_type=jnp.float32)
     residual = (x_cols.astype(jnp.float32) + attended).astype(jnp.bfloat16)
     rows_full = lax.all_gather(residual, "blk", axis=1, tiled=True)
     normed = rms_round(rows_full, mlp_gain)

time: 258 us -> 242 us (0.938)
  blocking collectives: 83.9 us -> 43.7 us
  waiting for transfers between devices: 111 us -> 124 us
  starting transfers between devices: 0.01 us -> 11.5 us
    all_gather x1 -> x0, blocking collectives: 45.3 us -> none  [body(): lax.all_gather(value_rows, 'blk', axis=0, tiled=True)]
    ppermute x0 -> x4, waiting for transfers between devices: none -> 14.6 us  [collect(): theirs = lax.ppermute(grown, axis, [(d, d ^ reach) for d in range(ways)])]
    ppermute x0 -> x4, starting transfers between devices: none -> 11.5 us  [collect(): theirs = lax.ppermute(grown, axis, [(d, d ^ reach) for d in range(ways)])]
    all_gather x1, blocking collectives: 38.5 us -> 43.7 us  [body(): rows_full = lax.all_gather(residual, 'blk', axis=1, tiled=True)]
  transfers between devices with their start and end apart: 2 -> 6, of which waited for: 2 -> 6; matrix products, arithmetic and copies ran while one was open for 1% -> 1% of each run, Pallas kernels for 0% -> 0%
where the time goes in v1:
time: 242 us; the launch traced here: 241 us
  waiting for transfers between devices  124 us (51%)
  blocking collectives  43.7 us (18%)
  matrix products  28.9 us (12%)
  between operations  13.6 us (6%)
  starting transfers between devices  11.5 us (5%)
  local copies, waits for them, and re-layouts  10.7 us (4%)
  other arithmetic  9.36 us (4%)
    psum x1, waiting for transfers between devices, body(): summed = lax.psum(partial_sum, 'blk')  108 us
    all_gather x1, blocking collectives, body(): rows_full = lax.all_gather(residual, 'blk', axis=1, tiled=True)  43.7 us
    dot_general x1, matrix products, body(): jnp.dot(rms_round(after_mlp, head_gain), w_head, preferred_element_type=j...  14.7 us
    ppermute x4, waiting for transfers between devices, collect(): theirs = lax.ppermute(grown, axis, [(d, d ^ reach) for d in range(ways)])  14.6 us
    ppermute x4, starting transfers between devices, collect(): theirs = lax.ppermute(grown, axis, [(d, d ^ reach) for d in range(ways)])  11.5 us
    dot_general x1, matrix products, body(): partial_sum = jnp.dot(hidden, w_down, preferred_element_type=jnp.float32)  5.04 us
  transfers between devices with their start and end apart: 6, of which 6 were waited for; matrix products, arithmetic and copies ran while one was open for 1% of the time, Pallas kernels for 0%

profile of v1, /device:TPU:0, one launch (start us, length us, event | category | flops | bytes accessed | tf_op | source)
XLA Modules:
  0.0 241.3 jit_solution(14094927562323134686)
XLA Ops:
  6.5 1.2 reshape.73
  7.8 1.3 gather_fusion.2
  9.1 1.3 gather_fusion.3
  10.5 0.7 slice_convert_fusion
  11.2 0.9 fusion.50
  12.1 2.2 fusion.62
  14.3 0.2 fusion.45
  14.6 2.4 fusion.4
  17.0 0.5 fusion.11
  17.5 3.0 %collective-permute-start = (bf16[8,2048]{1,0:T(8,128)(2,1)S(1)}, bf16[8,2048]{1,0:T(8,128)(2,1)S(1)}, u32[]{:S(2)}, u32[]{:S(2)}) collective-permute-start(bf16[8,2048]{1,0:T(8,128)(2,1)S(1)} %fusion.11), channel_id=1, source_target_pairs={{0,1},{1,0},{2,3},{3,2},{4,5},{5,4},{6,7},{7,6},{8,9},{9,8},{10,11... | collective-permute-start | bytes 98312 | tf_op jit(solution)/shard_map/ppermute | solution.py:13
  20.5 1.9 collective-permute-done
  22.4 2.1 collective-permute-start.1
  24.5 2.2 collective-permute-done.1
  26.8 2.1 collective-permute-start.2
  28.9 2.9 %collective-permute-done.2 = bf16[32,2048]{1,0:T(8,128)(2,1)S(1)} collective-permute-done((bf16[32,2048]{1,0:T(8,128)(2,1)S(1)}, bf16[32,2048]{1,0:T(8,128)(2,1)S(1)}, u32[]{:S(2)}, u32[]{:S(2)}) %collective-permute-start.2) | collective-permute-done | bytes 131104 | tf_op jit(solution)/shard_map/ppermute | solution.py:13
  31.9 4.2 %collective-permute-start.3 = (bf16[64,2048]{1,0:T(8,128)(2,1)S(1)}, bf16[64,2048]{1,0:T(8,128)(2,1)}, u32[]{:S(2)}, u32[]{:S(2)}) collective-permute-start(bf16[64,2048]{1,0:T(8,128)(2,1)S(1)} %maximum_select_fusion.2), channel_id=1, source_target_pairs={{0,8},{1,9},{2,10},{3,11},{4,12},{5,13},{6,14},{7,15},{8,0},{9,1},... | collective-permute-start | bytes 786440 | tf_op jit(solution)/shard_map/ppermute | solution.py:13
  36.1 7.5 %collective-permute-done.3 = bf16[64,2048]{1,0:T(8,128)(2,1)} collective-permute-done((bf16[64,2048]{1,0:T(8,128)(2,1)S(1)}, bf16[64,2048]{1,0:T(8,128)(2,1)}, u32[]{:S(2)}, u32[]{:S(2)}) %collective-permute-start.3) | collective-permute-done | bytes 262176 | tf_op jit(solution)/shard_map/ppermute | solution.py:13
  43.6 1.5 fusion.10
  45.1 43.7 %all_gather.3 = bf16[128,2048]{1,0:T(8,128)(2,1)S(1)} all-gather(bf16[128,128]{1,0:T(8,128)(2,1)S(1)} %fusion.10), channel_id=1, replica_groups=mesh['guide'=2,'blk'=16] {'blk'}, dimensions={1}, use_global_device_ids=true | all-gather | bytes 557056 | tf_op jit(solution)/shard_map/all_gather | solution.py:92
  88.8 0.2 fusion.15
  89.0 1.7 fusion.40
  90.7 5.0 %fusion.8 = f32[128,2048]{1,0:T(8,128)} fusion(bf16[684,2048]{1,0:T(8,128)(2,1)S(1)} %copy-done, bf16[2048,684]{0,1:T(8,128)(2,1)} %param.28, f32[128,684]{0,1:T(8,128)} %fusion.40, pred[684]{0:T(1024)(128)(4,1)S(1)} %add_compare_fusion, bf16[128,2048]{1,0:T(8,128)(2,1)S(1)} %all_gather.3, f32[2048]{0:T(1024)S(1)} %copy-done.6, f32[128]{0:T(128)S(1)} %add_rsqrt_fusion.1), kind=kOutput, calls=%fused_computation.21 | convolution fusion | flops 718887424 | bytes 7535788 | tf_op jit(solution)/shard_map/dot_general | solution.py:101
  95.8 107.8 %all-reduce.2.cloned.1.call-done = f32[128,2048]{1,0:T(8,128)} async-done(((f32[128,2048]{1,0:T(8,128)}), f32[128,2048]{1,0:T(8,128)}) %all-reduce.2.cloned.1.call-update) | async-done | bytes 1048592 | tf_op jit(solution)/shard_map/psum | solution.py:102
  203.6 1.5 fusion.12
  205.1 14.7 %fusion.63 = (bf16[128,6400]{1,0:T(8,128)(2,1)}, f32[128,6400]{1,0:T(8,128)}) fusion(bf16[2048,6400]{1,0:T(8,128)(2,1)} %param.31, f32[2048]{0:T(1024)S(1)} %copy-done.5, f32[128]{0:T(128)S(1)} %add_rsqrt_fusion, f32[128,2048]{1,0:T(8,128)} %all-reduce.2.cloned.1.call-done, bf16[128,2048]{1,0:T(8,128)(2,1)S(1)} %all_gather.3), kind=kOutput, calls=%fused_computation.101 | convolution fusion | flops 3358097408 | bytes 32711168 | tf_op jit(solution)/shard_map/dot_general | solution.py:104
  219.8 1.2 scatter_custom_fusion
  220.9 1.2 gather_fusion
  222.2 0.1 compare_and_fusion
  222.3 1.3 collective-permute-done.4
  223.6 4.3 %fusion.3 = bf16[128,6400]{1,0:T(8,128)(2,1)} fusion(f32[128,6400]{1,0:T(8,128)} %get-tuple-element.13, bf16[128,6400]{1,0:T(8,128)(2,1)} %collective-permute-done.4, f32[128]{0:T(128)S(1)} %and_select_fusion.2, pred[]{:T(512)S(6)} %eq.16), kind=kLoop, calls=%fused_computation.10 | loop fusion | flops 5734400 | bytes 6554113 | tf_op jit(solution)/shard_map/convert_element_type | solution.py:117
  227.9 4.3 %gather_fusion.1 = bf16[64,6400]{1,0:T(8,128)(2,1)} fusion(bf16[128,6400]{1,0:T(8,128)(2,1)} %fusion.3, s32[1024]{0:T(1024)S(1)} %pad_clamp_fusion), kind=kCustom, calls=%fused_computation.3 | custom fusion | bytes 1638656 | tf_op jit(solution)/shard_map/jit(_take)/gather | solution.py:120
  232.2 2.2 broadcast_select_fusion
  (39 shorter events, 0.4 us)
Async XLA Ops:
  6.5 84.2 %copy-start = (bf16[684,2048]{1,0:T(8,128)(2,1)S(1)}, bf16[684,2048]{1,0:T(8,128)(2,1)}, u32[]{:S(2)}) copy-start(bf16[684,2048]{1,0:T(8,128)(2,1)} %param.29) | copy-start | bytes 8404996
  6.5 197.0 %all-reduce.2.cloned.1.call-start = ((), (), s32[]{:S(2)}) async-start(), calls=%async_computation | async-start | bytes 2097152 | tf_op jit(solution)/shard_map/psum | solution.py:102
  14.6 2.4 copy-start.4
  14.6 29.0 %copy-start.7 = (bf16[128,128]{1,0:T(8,128)(2,1)S(1)}, bf16[128,128]{1,0:T(8,128)(2,1)}, u32[]{:S(2)}) copy-start(bf16[128,128]{1,0:T(8,128)(2,1)} %param.17) | copy-start | bytes 98308
  17.5 71.5 %copy-start.6 = (f32[2048]{0:T(1024)S(1)}, f32[2048]{0:T(1024)}, u32[]{:S(2)}) copy-start(f32[2048]{0:T(1024)} %param.26) | copy-start | bytes 24580
  17.5 4.9 %collective-permute-start = (bf16[8,2048]{1,0:T(8,128)(2,1)S(1)}, bf16[8,2048]{1,0:T(8,128)(2,1)S(1)}, u32[]{:S(2)}, u32[]{:S(2)}) collective-permute-start(bf16[8,2048]{1,0:T(8,128)(2,1)S(1)} %fusion.11), channel_id=1, source_target_pairs={{0,1},{1,0},{2,3},{3,2},{4,5},{5,4},{6,7},{7,6},{8,9},{9,8},{10,11... | collective-permute-start | bytes 98312 | tf_op jit(solution)/shard_map/ppermute | solution.py:13
  22.4 4.4 %collective-permute-start.1 = (bf16[16,2048]{1,0:T(8,128)(2,1)S(1)}, bf16[16,2048]{1,0:T(8,128)(2,1)S(1)}, u32[]{:S(2)}, u32[]{:S(2)}) collective-permute-start(bf16[16,2048]{1,0:T(8,128)(2,1)S(1)} %maximum_select_fusion.4), channel_id=1, source_target_pairs={{0,2},{1,3},{2,0},{3,1},{4,6},{5,7},{6,4},{7,5},{8,10},{9,11},{10,... | collective-permute-start | bytes 196616 | tf_op jit(solution)/shard_map/ppermute | solution.py:13
  26.8 5.1 %collective-permute-start.2 = (bf16[32,2048]{1,0:T(8,128)(2,1)S(1)}, bf16[32,2048]{1,0:T(8,128)(2,1)S(1)}, u32[]{:S(2)}, u32[]{:S(2)}) collective-permute-start(bf16[32,2048]{1,0:T(8,128)(2,1)S(1)} %maximum_select_fusion.3), channel_id=1, source_target_pairs={{0,4},{1,5},{2,6},{3,7},{4,0},{5,1},{6,2},{7,3},{8,12},{9,13},{10,... | collective-permute-start | bytes 393224 | tf_op jit(solution)/shard_map/ppermute | solution.py:13
  31.9 11.7 %collective-permute-start.3 = (bf16[64,2048]{1,0:T(8,128)(2,1)S(1)}, bf16[64,2048]{1,0:T(8,128)(2,1)}, u32[]{:S(2)}, u32[]{:S(2)}) collective-permute-start(bf16[64,2048]{1,0:T(8,128)(2,1)S(1)} %maximum_select_fusion.2), channel_id=1, source_target_pairs={{0,8},{1,9},{2,10},{3,11},{4,12},{5,13},{6,14},{7,15},{8,0},{9,1},... | collective-permute-start | bytes 786440 | tf_op jit(solution)/shard_map/ppermute | solution.py:13
  36.1 52.9 %copy-start.3 = (bf16[2048,684]{0,1:T(8,128)(2,1)S(1)}, bf16[2048,684]{0,1:T(8,128)(2,1)}, u32[]{:S(2)}) copy-start(bf16[2048,684]{0,1:T(8,128)(2,1)} %param.27) | copy-start | bytes 8404996
  90.7 114.3 %copy-start.5 = (f32[2048]{0:T(1024)S(1)}, f32[2048]{0:T(1024)}, u32[]{:S(2)}) copy-start(f32[2048]{0:T(1024)} %param.30) | copy-start | bytes 24580
  205.1 14.7 %copy-start.2 = (s32[128]{0:T(128)S(1)}, s32[128]{0:T(128)}, u32[]{:S(2)}) copy-start(s32[128]{0:T(128)} %param.22) | copy-start | bytes 1540
  205.1 15.9 %copy-start.1 = (f32[128]{0:T(128)S(1)}, f32[128]{0:T(128)}, u32[]{:S(2)}) copy-start(f32[128]{0:T(128)} %param.23) | copy-start | bytes 1540
  219.7 3.8 %collective-permute-start.4 = (bf16[128,6400]{1,0:T(8,128)(2,1)}, bf16[128,6400]{1,0:T(8,128)(2,1)}, u32[]{:S(2)}, u32[]{:S(2)}) collective-permute-start(bf16[128,6400]{1,0:T(8,128)(2,1)} %get-tuple-element.12), channel_id=1, source_target_pairs={{0,16},{16,0},{1,17},{17,1},{2,18},{18,2},{3,19},{19,3},{4,20},{20... | collective-permute-start | bytes 4915208 | tf_op jit(solution)/shard_map/ppermute | solution.py:24
Sparse Core Ops, SparseCore 0:
  95.9 107.6 all-reduce.1
